TPU v7x, 32 devices: a whole 2x2x4 slice. The times are simulated.
32 devices in a mesh: group: 4 (over x, core), tensor: 4 (over z), dp: 2 (over y).
Axes of the slice: x: 2, y: 2, z: 4, core: 2. Of those that a mesh axis runs over, the one named last changes fastest.
Arguments:
- doc_emb: bfloat16 [48, 4096], P('group', 'dp'), may hold values from -6 to 6
- row_emb: bfloat16 [64, 4096], P(None, 'dp'), may hold values from -6 to 6
- hyper_in: bfloat16 [4096, 8192], P('dp', 'tensor'), may hold values from -0.09375 to 0.09375
- hyper_out: bfloat16 [8192, 8192], P('tensor', 'dp'), may hold values from -0.0625 to 0.0625
- assign: int32 [48], replicated, may hold values from 0 to 47, each once
- states: bfloat16 [2304, 8192], P('group', 'tensor'), may hold values from -6 to 6
- proj_weight: bfloat16 [8192, 8192], P('tensor', 'dp'), may hold values from -0.0625 to 0.0625
- targets: bfloat16 [2304, 8192], P(('group', 'tensor'), 'dp'), may hold values from -6 to 6
Outputs:
- adapted: bfloat16 [2304, 8192], P(('group', 'tensor'), 'dp')
- grad_down: float32 [48, 32, 8192], P('group', None, 'tensor')
- grad_up: float32 [48, 32, 8192], P('group', None, ('dp', 'tensor'))
Inputs may be any that keep to these rules, and one draw needn't show every extreme that they name: `assign`: every document is named by exactly one slot.
All inputs are finite; a program needn't handle non-finite values.
Results may differ from a plain program's by a relative error of at most 0.02.
Values may be sent and summed in bfloat16 or wider, within the bound.
No kernel may reach another device: no remote copies, remote signals or barrier semaphores. Data moves between devices by JAX's collectives and lax.ppermute only.
A program may use at most 128 MiB of HBM per device.

v0:
```python
import math
import jax
import jax.numpy as jnp
from jax import lax
from jax.sharding import PartitionSpec as P

D = 8192
R = 32
LOWDIM_MULTIPLE = 0.1


def spread(block, axis, owner):
    block = jnp.where(lax.axis_index(axis) == owner, block, jnp.zeros_like(block))
    return lax.psum(block, axis)


def hypernet(doc_rows, row_emb, hyper_in, hyper_out):
    doc_count = doc_rows.shape[0]
    pre_doc, pre_row = (
        lax.psum(
            jnp.dot(doc_rows, hyper_in, preferred_element_type=jnp.float32).astype(jnp.bfloat16),
            "dp",
        ).astype(jnp.float32),
        lax.psum(
            jnp.dot(row_emb, hyper_in, preferred_element_type=jnp.float32).astype(jnp.bfloat16),
            "dp",
        ).astype(jnp.float32),
    )
    hidden = jax.nn.silu(pre_doc[:, None, :] + pre_row[None, :, :]).astype(jnp.bfloat16)
    hidden = hidden.reshape(doc_count * 2 * R, hidden.shape[2])
    partial_value = jnp.dot(hidden, hyper_out, preferred_element_type=jnp.float32)
    summed = lax.psum(partial_value.astype(jnp.bfloat16), "tensor")
    factors = summed.reshape(doc_count, 2 * R, hyper_out.shape[1])
    ratio_axes = lax.axis_size("tensor") // lax.axis_size("dp")
    owner_rows = spread(factors[:, :R, :], "dp", lax.axis_index("tensor") // ratio_axes)
    col_width = hyper_out.shape[1] // ratio_axes
    down_block = lax.dynamic_slice_in_dim(
        owner_rows, lax.axis_index("tensor") % ratio_axes * col_width, col_width, 2
    )
    return (down_block, factors[:, R:, :])


def body(doc_emb, row_emb, hyper_in, hyper_out, assign, states, proj_weight, targets):
    doc_count = doc_emb.shape[0]
    group_start = lax.axis_index("group") * doc_count
    slot_docs = lax.dynamic_slice_in_dim(assign, group_start, doc_count)
    everyone = lax.all_gather(doc_emb, "group", axis=0, tiled=True)
    picker = (slot_docs[:, None] == jnp.arange(everyone.shape[0], dtype=jnp.int32)[None, :]).astype(
        jnp.bfloat16
    )
    chosen = jnp.dot(picker, everyone, preferred_element_type=jnp.float32).astype(jnp.bfloat16)
    slot_down, slot_up_factor = hypernet(chosen, row_emb, hyper_in, hyper_out)
    token_count = states.shape[0]
    per_doc = token_count // doc_count
    fan_width_multiplier = 1.0 / math.sqrt(D)
    bundled_entries = states.reshape(doc_count, per_doc, states.shape[1])
    low_part = jnp.einsum(
        "quw,qlw->qul", bundled_entries, slot_down, preferred_element_type=jnp.float32
    ).reshape(token_count, R)
    base_part = jnp.dot(states, proj_weight, preferred_element_type=jnp.float32)
    frozen_output, low_sum = (
        lax.psum_scatter(
            base_part.astype(jnp.bfloat16), "tensor", scatter_dimension=0, tiled=True
        ).astype(jnp.float32),
        lax.psum_scatter(
            low_part.astype(jnp.bfloat16), "tensor", scatter_dimension=0, tiled=True
        ).astype(jnp.float32),
    )
    row_count = frozen_output.shape[0]
    row_start = lax.axis_index("tensor") * row_count
    owner_doc = (row_start + jnp.arange(row_count, dtype=jnp.int32)) // per_doc
    document_member = owner_doc[:, None] == jnp.arange(doc_count, dtype=jnp.int32)[None, :]
    narrow_basis_map = (low_sum * fan_width_multiplier).astype(jnp.bfloat16)
    broadcast_rows = jnp.where(
        document_member[:, :, None], narrow_basis_map[:, None, :], jnp.zeros((), jnp.bfloat16)
    ).reshape(row_count, doc_count * R)
    up_factor_rows = slot_up_factor.reshape(doc_count * R, slot_up_factor.shape[2])
    raised_rows = frozen_output + LOWDIM_MULTIPLE * jnp.dot(
        broadcast_rows, up_factor_rows, preferred_element_type=jnp.float32
    )
    adapted = raised_rows.astype(jnp.bfloat16)
    residual = (raised_rows - targets.astype(jnp.float32)).astype(jnp.bfloat16)
    partial_up_gradient = LOWDIM_MULTIPLE * lax.dot_general(
        broadcast_rows, residual, (((0,), (0,)), ((), ())), preferred_element_type=jnp.float32
    )
    grad_up_local = lax.psum_scatter(
        partial_up_gradient.reshape(doc_count, R, up_factor_rows.shape[1]).astype(jnp.bfloat16),
        "tensor",
        scatter_dimension=2,
        tiled=True,
    ).astype(jnp.float32)
    document_list = lax.dot_general(
        residual, up_factor_rows, (((1,), (1,)), ((), ())), preferred_element_type=jnp.float32
    ).reshape(row_count, doc_count, R)
    token_portion = LOWDIM_MULTIPLE * jnp.sum(
        jnp.where(document_member[:, :, None], document_list, 0.0), axis=1
    )
    placed = lax.dynamic_update_slice_in_dim(
        jnp.zeros((token_count, R), jnp.float32), token_portion, row_start, 0
    )
    position_sensitivity = lax.psum(placed, ("tensor", "dp")).astype(jnp.bfloat16)
    lowering_matrix_sensitivity = fan_width_multiplier * jnp.einsum(
        "oed,oec->odc",
        position_sensitivity.reshape(doc_count, per_doc, R),
        bundled_entries,
        preferred_element_type=jnp.float32,
    )
    own_docs = group_start + jnp.arange(doc_count, dtype=jnp.int32)
    initial_grads = (
        jnp.zeros(
            (
                doc_count,
                lowering_matrix_sensitivity.shape[1] * lowering_matrix_sensitivity.shape[2],
            ),
            jnp.float32,
        ),
        jnp.zeros((doc_count, grad_up_local.shape[1] * grad_up_local.shape[2]), jnp.float32),
    )
    pieces = (
        lax.all_gather(
            lowering_matrix_sensitivity.astype(jnp.bfloat16), "group", axis=0, tiled=True
        ).astype(jnp.float32),
        lax.all_gather(grad_up_local.astype(jnp.bfloat16), "group", axis=0, tiled=True).astype(
            jnp.float32
        ),
    )
    piece_rows = pieces[0].shape[0]
    picker = (own_docs[:, None] == assign[None, :]).astype(jnp.float32)
    first = initial_grads[0] + jnp.dot(
        picker, pieces[0].reshape(piece_rows, -1), precision=lax.Precision.HIGHEST
    )
    second = initial_grads[1] + jnp.dot(
        picker, pieces[1].reshape(piece_rows, -1), precision=lax.Precision.HIGHEST
    )
    grad_down = first.reshape(lowering_matrix_sensitivity.shape)
    grad_up = second.reshape(grad_up_local.shape)
    return (adapted, grad_down, grad_up)


def solution(mesh):
    in_specs = (
        P("group", "dp"),
        P(None, "dp"),
        P("dp", "tensor"),
        P("tensor", "dp"),
        P(),
        P("group", "tensor"),
        P("tensor", "dp"),
        P(("group", "tensor"), "dp"),
    )
    out_specs = (
        P(("group", "tensor"), "dp"),
        P("group", None, "tensor"),
        P("group", None, ("dp", "tensor")),
    )
    return jax.shard_map(body, mesh=mesh, in_specs=in_specs, out_specs=out_specs, check_vma=False)
```

profile of v0, /device:TPU:0, one launch (start us, length us, event | category | flops | bytes accessed | tf_op | source)
XLA Modules:
  0.0 643.9 jit_solution(16494009230367694234)
XLA Ops:
  7.2 5.9 convolution_convert_fusion.2
  13.2 7.2 %all-gather = bf16[4,12,2048]{2,1,0:T(8,128)(2,1)S(1)} all-gather(bf16[1,12,2048]{2,1,0:T(8,128)(2,1)S(1)} %bitcast.83), channel_id=1, replica_groups=mesh['group'=4,'tensor'=4,'dp'=2] {'group'}, dimensions={0}, use_global_device_ids=true | all-gather | bytes 245760 | tf_op jit(solution)/shard_map/all_gather | solution.py:47
  20.6 4.8 convolution_convert_fusion.4
  25.4 8.9 %psum.35 = bf16[12,2048]{1,0:T(8,128)(2,1)S(1)} all-reduce(bf16[12,2048]{1,0:T(8,128)(2,1)S(1)} %convolution_convert_fusion.4), channel_id=1, replica_groups=mesh['group'=4,'tensor'=4,'dp'=2] {'dp'}, use_global_device_ids=true, to_apply=%region_1.0 | all-reduce | flops 24576 | bytes 98304 | tf_op jit(solution)/shard_map/psum | solution.py:20
  34.3 5.0 all-reduce.4.cloned.1.call-done
  39.3 1.0 convert_element_type.76
  40.3 0.8 broadcast_add_fusion
  41.1 1.7 fusion.6
  42.8 18.5 %convolution_convert_fusion = bf16[768,4096]{1,0:T(8,128)(2,1)} fusion(bf16[768,2048]{1,0:T(8,128)(2,1)S(1)} %fusion.6, bf16[2048,4096]{1,0:T(8,128)(2,1)} %param.11), kind=kOutput, calls=%fused_computation | convolution fusion | flops 12888047616 | bytes 26214400 | tf_op jit(solution)/shard_map/dot_general | solution.py:31
  61.4 222.9 %all-reduce.6.cloned.1.call-done = bf16[12,64,4096]{2,1,0:T(8,128)(2,1)} async-done(((bf16[12,64,4096]{2,1,0:T(8,128)(2,1)}), bf16[12,64,4096]{2,1,0:T(8,128)(2,1)}) %all-reduce.6.cloned.1.call-update) | async-done | bytes 6291472 | tf_op jit(solution)/shard_map/psum | solution.py:32
  284.4 3.8 slice_select_fusion
  288.2 84.8 %all-reduce.8.cloned.1.call-done = bf16[12,32,4096]{2,1,0:T(8,128)(2,1)} async-done(((bf16[12,32,4096]{2,1,0:T(8,128)(2,1)}), bf16[12,32,4096]{2,1,0:T(8,128)(2,1)}) %all-reduce.8.cloned.1.call-update) | async-done | bytes 3145744 | tf_op jit(solution)/shard_map/psum | solution.py:14
  373.0 2.1 fusion.31
  375.2 0.8 copy.27
  376.2 15.0 %convolution_convert_fusion.1 = bf16[576,4096]{1,0:T(8,128)(2,1)} fusion(bf16[576,2048]{1,0:T(8,128)(2,1)S(1)} %copy-done, bf16[2048,4096]{1,0:T(8,128)(2,1)} %param.14), kind=kOutput, calls=%fused_computation.11 | convolution fusion | flops 9666035712 | bytes 23855104 | tf_op jit(solution)/shard_map/dot_general | solution.py:60
  391.3 4.4 reduce-scatter.10.cloned.1.call-done
  395.7 0.8 copy.26
  396.5 0.7 broadcast_select_fusion
  397.2 84.1 %reduce-scatter.6.cloned.1.call-done = bf16[144,4096]{1,0:T(8,128)(2,1)} async-done(((bf16[576,4096]{1,0:T(8,128)(2,1)}), bf16[144,4096]{1,0:T(8,128)(2,1)}) %reduce-scatter.6.cloned.1.call-update) | async-done | bytes 1179664 | tf_op jit(solution)/shard_map/reduce_scatter | solution.py:62
  481.4 4.1 fusion.47
  485.5 2.7 multiply_convert_fusion
  488.2 0.6 copy-done.6
  488.8 3.6 fusion.23
  492.9 40.6 %psum.39 = bf16[576,32]{0,1:T(8,128)(2,1)S(1)} all-reduce(f32[576,32]{0,1:T(8,128)S(1)} %dynamic_update_slice.3), channel_id=1, replica_groups=mesh['group'=4,'tensor'=4,'dp'=2] {'tensor','dp'}, use_global_device_ids=true, to_apply=%region_7.8 | all-reduce | flops 18432 | bytes 110592 | tf_op jit(solution)/shard_map/psum | solution.py:101
  533.7 1.7 multiply_convert_fusion.1
  535.7 15.1 %reduce-scatter.8.cloned.1.call-done = bf16[12,32,1024]{2,1,0:T(8,128)(2,1)} async-done(((bf16[12,32,4096]{2,1,0:T(8,128)(2,1)}), bf16[12,32,1024]{2,1,0:T(8,128)(2,1)}) %reduce-scatter.8.cloned.1.call-update) | async-done | bytes 786448 | tf_op jit(solution)/shard_map/reduce_scatter | solution.py:86
  550.8 48.7 %all-gather.4.cloned.1.call-done = bf16[48,32,2048]{2,1,0:T(8,128)(2,1)} async-done(((bf16[12,32,2048]{2,1,0:T(8,128)(2,1)}), bf16[48,32,2048]{2,1,0:T(8,128)(2,1)}) %all-gather.4.cloned.1.call-update) | async-done | bytes 6291472 | tf_op jit(solution)/shard_map/all_gather | solution.py:120
  599.6 9.6 %fusion = f32[12,32,2048]{2,0,1:T(8,128)S(1)} fusion(s32[48]{0:T(128)S(1)} %copy-done.8, s32[12]{0:T(128)S(1)} %iota_add_fusion, bf16[6,8,32,2048]{3,2,1,0:T(8,128)(2,1)} %bitcast.79), kind=kOutput, calls=%fused_computation.1 | convolution fusion | flops 75498048 | bytes 9437424 | tf_op jit(solution)/shard_map/dot_general | solution.py:129
  609.1 3.5 copy.23
  612.6 17.1 %all-gather.6.cloned.1.call-done = bf16[48,32,1024]{2,1,0:T(8,128)(2,1)} async-done(((bf16[12,32,1024]{2,1,0:T(8,128)(2,1)}), bf16[48,32,1024]{2,1,0:T(8,128)(2,1)}) %all-gather.6.cloned.1.call-update) | async-done | bytes 3145744 | tf_op jit(solution)/shard_map/all_gather | solution.py:123
  629.7 5.3 fusion.9
  635.0 2.1 copy.24
  (44 shorter events, 1.7 us)
Async XLA Ops:
  7.2 365.9 %copy-start = (bf16[576,2048]{1,0:T(8,128)(2,1)S(1)}, bf16[576,2048]{1,0:T(8,128)(2,1)}, u32[]{:S(2)}) copy-start(bf16[576,2048]{1,0:T(8,128)(2,1)} %param.13) | copy-start | bytes 7077892
  7.2 6.0 copy-start.4
  7.2 13.3 %copy-start.7 = (s32[48]{0:T(128)S(1)}, s32[48]{0:T(128)}, u32[]{:S(2)}) copy-start(s32[48]{0:T(128)} %param.12) | copy-start | bytes 580
  7.2 32.1 %all-reduce.4.cloned.1.call-start = ((), (), s32[]{:S(2)}) async-start(), calls=%async_computation.4 | async-start | bytes 524288 | tf_op jit(solution)/shard_map/psum | solution.py:24
  13.2 271.2 %all-reduce.6.cloned.1.call-start = ((), (), s32[]{:S(2)}) async-start(), calls=%async_computation.5 | async-start | bytes 12582912 | tf_op jit(solution)/shard_map/psum | solution.py:32
  61.4 311.7 %all-reduce.8.cloned.1.call-start = ((), (), s32[]{:S(2)}) async-start(), calls=%async_computation.6 | async-start | bytes 6291456 | tf_op jit(solution)/shard_map/psum | solution.py:14
  288.1 107.5 %reduce-scatter.10.cloned.1.call-start = ((), (), s32[]{:S(2)}) async-start(), calls=%async_computation.10 | async-start | bytes 184320
  376.0 105.4 %reduce-scatter.6.cloned.1.call-start = ((), (), s32[]{:S(2)}) async-start(), calls=%async_computation.3 | async-start | bytes 5898240 | tf_op jit(solution)/shard_map/reduce_scatter | solution.py:62
  391.2 159.6 %reduce-scatter.8.cloned.1.call-start = ((), (), s32[]{:S(2)}) async-start(), calls=%async_computation.8 | async-start | bytes 3932160 | tf_op jit(solution)/shard_map/reduce_scatter | solution.py:86
  391.3 5.3 copy-start.5
  397.2 88.2 %copy-start.2 = (bf16[144,4096]{1,0:T(8,128)(2,1)S(1)}, bf16[144,4096]{1,0:T(8,128)(2,1)}, u32[]{:S(2)}) copy-start(bf16[144,4096]{1,0:T(8,128)(2,1)} %param.15) | copy-start | bytes 3538948
  481.4 4.1 copy-start.3
  485.5 2.7 copy-start.1
  488.2 0.7 copy-start.6
  488.2 111.4 %all-gather.4.cloned.1.call-start = ((), (), s32[]{:S(2)}) async-start(), calls=%async_computation.7 | async-start | bytes 7864320 | tf_op jit(solution)/shard_map/all_gather | solution.py:120
  533.7 65.9 %copy-start.8 = (s32[48]{0:T(128)S(1)}, s32[48]{0:T(128)}, u32[]{:S(2)}) copy-start(s32[48]{0:T(128)} %param.12) | copy-start | bytes 580
  535.4 94.2 %all-gather.6.cloned.1.call-start = ((), (), s32[]{:S(2)}) async-start(), calls=%async_computation.9 | async-start | bytes 3932160 | tf_op jit(solution)/shard_map/all_gather | solution.py:123
Sparse Core Ops, SparseCore 0:
  13.3 26.0 all-reduce.3
  61.5 222.8 all-reduce.5
  288.3 84.7 all-reduce.7
  376.1 19.5 reduce-scatter.9
  397.8 83.4 reduce-scatter.5
  488.3 62.4 reduce-scatter.7
  552.9 46.5 all-gather.3
  601.1 28.4 all-gather.5
where the time goes:
time: 644 us
  waiting for transfers between devices  482 us (75%)
  matrix products  73.3 us (11%)
  blocking collectives  56.7 us (9%)
  between operations  14.4 us (2%)
  local copies, waits for them, and re-layouts  8.55 us (1%)
  other arithmetic  7.99 us (1%)
    psum x1, waiting for transfers between devices, hypernet(): summed = lax.psum(partial_value.astype(jnp.bfloat16), 'tensor')  223 us
    psum x1, waiting for transfers between devices, spread(): return lax.psum(block, axis)  84.8 us
    reduce_scatter x1, waiting for transfers between devices, body(): lax.psum_scatter(base_part.astype(jnp.bfloat16), 'tensor', scatter_dimens...  84.1 us
    all_gather x1, waiting for transfers between devices, body(): lax.all_gather(lowering_matrix_sensitivity.astype(jnp.bfloat16), 'group',...  48.7 us
    psum x1, blocking collectives, body(): lax.psum(placed, ('tensor', 'dp')).astype(jnp.bfloat16)  40.6 us
    dot_general x1, matrix products, hypernet(): jnp.dot(hidden, hyper_out, preferred_element_type=jnp.float32)  18.5 us
    all_gather x1, waiting for transfers between devices, body(): lax.all_gather(grad_up_local.astype(jnp.bfloat16), 'group', axis=0, tiled...  17.1 us
    reduce_scatter x1, waiting for transfers between devices, body(): lax.psum_scatter(partial_up_gradient.reshape(doc_count, R, up_factor_rows...  15.1 us
  transfers between devices with their start and end apart: 8, of which 8 were waited for; matrix products, arithmetic and copies ran while one was open for 6% of the time, Pallas kernels for 0%

commit v1 on v0

--- a/solution.py
+++ b/solution.py
@@ -117,8 +117,16 @@
         jnp.zeros((doc_count, grad_up_local.shape[1] * grad_up_local.shape[2]), jnp.float32),
     )
     pieces = (
-        lax.all_gather(
-            lowering_matrix_sensitivity.astype(jnp.bfloat16), "group", axis=0, tiled=True
+        jnp.concatenate(
+            lax.all_to_all(
+                jnp.stack(
+                    [lowering_matrix_sensitivity.astype(jnp.bfloat16)] * lax.axis_size("group")
+                ),
+                "group",
+                0,
+                0,
+            ),
+            axis=0,
         ).astype(jnp.float32),
         lax.all_gather(grad_up_local.astype(jnp.bfloat16), "group", axis=0, tiled=True).astype(
             jnp.float32

time: 644 us -> 658 us (1.022)
  waiting for transfers between devices: 482 us -> 489 us
    all_to_all x0 -> x1, waiting for transfers between devices: none -> 79.8 us  [body(): lax.all_to_all(jnp.stack([lowering_matrix_sensitivity.astype(jnp.bfloat16...]
    all_gather x1 -> x0, waiting for transfers between devices: 48.7 us -> none  [body(): lax.all_gather(lowering_matrix_sensitivity.astype(jnp.bfloat16), 'group',...]
    all_gather x1, waiting for transfers between devices: 17.1 us -> 0.01 us  [body(): lax.all_gather(grad_up_local.astype(jnp.bfloat16), 'group', axis=0, tiled...]
    reduce_scatter x1, waiting for transfers between devices: 15.1 us -> 7.43 us  [body(): lax.psum_scatter(partial_up_gradient.reshape(doc_count, R, up_factor_rows...]
  transfers between devices with their start and end apart: 8 -> 8, of which waited for: 8 -> 7; matrix products, arithmetic and copies ran while one was open for 6% -> 6% of each run, Pallas kernels for 0% -> 0%
where the time goes in v1:
time: 658 us
  waiting for transfers between devices  489 us (74%)
  matrix products  72.1 us (11%)
  blocking collectives  56.7 us (9%)
  between operations  14.4 us (2%)
  local copies, waits for them, and re-layouts  12 us (2%)
  other arithmetic  7.99 us (1%)
    psum x1, waiting for transfers between devices, hypernet(): summed = lax.psum(partial_value.astype(jnp.bfloat16), 'tensor')  223 us
    psum x1, waiting for transfers between devices, spread(): return lax.psum(block, axis)  84.8 us
    reduce_scatter x1, waiting for transfers between devices, body(): lax.psum_scatter(base_part.astype(jnp.bfloat16), 'tensor', scatter_dimens...  84.1 us
    all_to_all x1, waiting for transfers between devices, body(): lax.all_to_all(jnp.stack([lowering_matrix_sensitivity.astype(jnp.bfloat16...  79.8 us
    psum x1, blocking collectives, body(): lax.psum(placed, ('tensor', 'dp')).astype(jnp.bfloat16)  40.6 us
    dot_general x1, matrix products, hypernet(): jnp.dot(hidden, hyper_out, preferred_element_type=jnp.float32)  18.5 us
    dot_general x1, matrix products, body(): base_part = jnp.dot(states, proj_weight, preferred_element_type=jnp.float32)  15 us
  transfers between devices with their start and end apart: 8, of which 7 were waited for; matrix products, arithmetic and copies ran while one was open for 6% of the time, Pallas kernels for 0%

profile of v1, /device:TPU:0, one launch (start us, length us, event | category | flops | bytes accessed | tf_op | source)
XLA Modules:
  0.0 657.8 jit_solution(17882291807797755330)
XLA Ops:
  7.2 5.9 convolution_convert_fusion.2
  13.2 7.2 %all-gather = bf16[4,12,2048]{2,1,0:T(8,128)(2,1)S(1)} all-gather(bf16[1,12,2048]{2,1,0:T(8,128)(2,1)S(1)} %bitcast.83), channel_id=1, replica_groups=mesh['group'=4,'tensor'=4,'dp'=2] {'group'}, dimensions={0}, use_global_device_ids=true | all-gather | bytes 245760 | tf_op jit(solution)/shard_map/all_gather | solution.py:47
  20.6 4.8 convolution_convert_fusion.4
  25.4 8.9 %psum.35 = bf16[12,2048]{1,0:T(8,128)(2,1)S(1)} all-reduce(bf16[12,2048]{1,0:T(8,128)(2,1)S(1)} %convolution_convert_fusion.4), channel_id=1, replica_groups=mesh['group'=4,'tensor'=4,'dp'=2] {'dp'}, use_global_device_ids=true, to_apply=%region_1.0 | all-reduce | flops 24576 | bytes 98304 | tf_op jit(solution)/shard_map/psum | solution.py:20
  34.3 5.0 all-reduce.4.cloned.1.call-done
  39.3 1.0 convert_element_type.76
  40.3 0.8 broadcast_add_fusion
  41.1 1.7 fusion.6
  42.8 18.5 %convolution_convert_fusion = bf16[768,4096]{1,0:T(8,128)(2,1)} fusion(bf16[768,2048]{1,0:T(8,128)(2,1)S(1)} %fusion.6, bf16[2048,4096]{1,0:T(8,128)(2,1)} %param.11), kind=kOutput, calls=%fused_computation | convolution fusion | flops 12888047616 | bytes 26214400 | tf_op jit(solution)/shard_map/dot_general | solution.py:31
  61.4 222.9 %all-reduce.6.cloned.1.call-done = bf16[12,64,4096]{2,1,0:T(8,128)(2,1)} async-done(((bf16[12,64,4096]{2,1,0:T(8,128)(2,1)}), bf16[12,64,4096]{2,1,0:T(8,128)(2,1)}) %all-reduce.6.cloned.1.call-update) | async-done | bytes 6291472 | tf_op jit(solution)/shard_map/psum | solution.py:32
  284.3 3.8 slice_select_fusion
  288.2 84.8 %all-reduce.8.cloned.1.call-done = bf16[12,32,4096]{2,1,0:T(8,128)(2,1)} async-done(((bf16[12,32,4096]{2,1,0:T(8,128)(2,1)}), bf16[12,32,4096]{2,1,0:T(8,128)(2,1)}) %all-reduce.8.cloned.1.call-update) | async-done | bytes 3145744 | tf_op jit(solution)/shard_map/psum | solution.py:14
  373.0 2.1 fusion.31
  375.2 0.8 copy.27
  376.2 15.0 %convolution_convert_fusion.1 = bf16[576,4096]{1,0:T(8,128)(2,1)} fusion(bf16[576,2048]{1,0:T(8,128)(2,1)S(1)} %copy-done, bf16[2048,4096]{1,0:T(8,128)(2,1)} %param.14), kind=kOutput, calls=%fused_computation.11 | convolution fusion | flops 9666035712 | bytes 23855104 | tf_op jit(solution)/shard_map/dot_general | solution.py:60
  391.3 4.4 reduce-scatter.10.cloned.1.call-done
  395.7 0.8 copy.26
  396.5 0.7 broadcast_select_fusion
  397.2 84.1 %reduce-scatter.6.cloned.1.call-done = bf16[144,4096]{1,0:T(8,128)(2,1)} async-done(((bf16[576,4096]{1,0:T(8,128)(2,1)}), bf16[144,4096]{1,0:T(8,128)(2,1)}) %reduce-scatter.6.cloned.1.call-update) | async-done | bytes 1179664 | tf_op jit(solution)/shard_map/reduce_scatter | solution.py:62
  481.3 4.1 fusion.47
  485.4 2.7 multiply_convert_fusion
  488.1 0.7 copy-done.6
  488.8 3.6 fusion.23
  492.9 40.6 %psum.39 = bf16[576,32]{0,1:T(8,128)(2,1)S(1)} all-reduce(f32[576,32]{0,1:T(8,128)S(1)} %dynamic_update_slice.3), channel_id=1, replica_groups=mesh['group'=4,'tensor'=4,'dp'=2] {'tensor','dp'}, use_global_device_ids=true, to_apply=%region_7.8 | all-reduce | flops 18432 | bytes 110592 | tf_op jit(solution)/shard_map/psum | solution.py:101
  534.2 3.4 stack.2
  537.6 5.4 all-to-all-start
  543.3 7.4 %reduce-scatter.8.cloned.1.call-done = bf16[12,32,1024]{2,1,0:T(8,128)(2,1)} async-done(((bf16[12,32,4096]{2,1,0:T(8,128)(2,1)}), bf16[12,32,1024]{2,1,0:T(8,128)(2,1)}) %reduce-scatter.8.cloned.1.call-update) | async-done | bytes 786448 | tf_op jit(solution)/shard_map/reduce_scatter | solution.py:86
  550.7 79.8 %all-to-all-done = bf16[4,12,32,2048]{3,2,1,0:T(8,128)(2,1)} async-done(((bf16[4,12,32,2048]{3,2,1,0:T(8,128)(2,1)}), bf16[4,12,32,2048]{3,2,1,0:T(8,128)(2,1)}, u32[]{:S(2)}, u32[]{:S(2)}) %all-to-all-start) | async-done | bytes 6291488 | tf_op jit(solution)/shard_map/all_to_all | solution.py:121
  630.5 9.6 %fusion = f32[12,32,2048]{2,0,1:T(8,128)S(1)} fusion(s32[48]{0:T(128)S(1)} %copy-done.8, s32[12]{0:T(128)S(1)} %iota_add_fusion, bf16[6,8,32,2048]{3,2,1,0:T(8,128)(2,1)} %bitcast.20), kind=kOutput, calls=%fused_computation.1 | convolution fusion | flops 75498048 | bytes 9437424 | tf_op jit(solution)/shard_map/dot_general | solution.py:137
  640.1 3.5 copy.23
  643.6 5.3 fusion.9
  648.9 2.1 copy.24
  (44 shorter events, 2.2 us)
Async XLA Ops:
  7.2 365.8 %copy-start = (bf16[576,2048]{1,0:T(8,128)(2,1)S(1)}, bf16[576,2048]{1,0:T(8,128)(2,1)}, u32[]{:S(2)}) copy-start(bf16[576,2048]{1,0:T(8,128)(2,1)} %param.13) | copy-start | bytes 7077892
  7.2 6.0 copy-start.4
  7.2 13.3 %copy-start.7 = (s32[48]{0:T(128)S(1)}, s32[48]{0:T(128)}, u32[]{:S(2)}) copy-start(s32[48]{0:T(128)} %param.12) | copy-start | bytes 580
  7.2 32.1 %all-reduce.4.cloned.1.call-start = ((), (), s32[]{:S(2)}) async-start(), calls=%async_computation.5 | async-start | bytes 524288 | tf_op jit(solution)/shard_map/psum | solution.py:24
  13.2 271.2 %all-reduce.6.cloned.1.call-start = ((), (), s32[]{:S(2)}) async-start(), calls=%async_computation.6 | async-start | bytes 12582912 | tf_op jit(solution)/shard_map/psum | solution.py:32
  61.3 311.7 %all-reduce.8.cloned.1.call-start = ((), (), s32[]{:S(2)}) async-start(), calls=%async_computation.7 | async-start | bytes 6291456 | tf_op jit(solution)/shard_map/psum | solution.py:14
  288.1 107.5 %reduce-scatter.10.cloned.1.call-start = ((), (), s32[]{:S(2)}) async-start(), calls=%async_computation.10 | async-start | bytes 184320
  376.0 105.3 %reduce-scatter.6.cloned.1.call-start = ((), (), s32[]{:S(2)}) async-start(), calls=%async_computation.4 | async-start | bytes 5898240 | tf_op jit(solution)/shard_map/reduce_scatter | solution.py:62
  391.2 159.5 %reduce-scatter.8.cloned.1.call-start = ((), (), s32[]{:S(2)}) async-start(), calls=%async_computation.8 | async-start | bytes 3932160 | tf_op jit(solution)/shard_map/reduce_scatter | solution.py:86
  391.3 5.3 copy-start.5
  397.2 88.2 %copy-start.2 = (bf16[144,4096]{1,0:T(8,128)(2,1)S(1)}, bf16[144,4096]{1,0:T(8,128)(2,1)}, u32[]{:S(2)}) copy-start(bf16[144,4096]{1,0:T(8,128)(2,1)} %param.15) | copy-start | bytes 3538948
  481.3 4.1 copy-start.3
  485.4 2.7 copy-start.1
  488.1 0.7 copy-start.6
  537.6 92.9 %copy-start.8 = (s32[48]{0:T(128)S(1)}, s32[48]{0:T(128)}, u32[]{:S(2)}) copy-start(s32[48]{0:T(128)} %param.12) | copy-start | bytes 580
  537.6 92.9 %all-to-all-start = ((bf16[4,12,32,2048]{3,2,1,0:T(8,128)(2,1)}), bf16[4,12,32,2048]{3,2,1,0:T(8,128)(2,1)}, u32[]{:S(2)}, u32[]{:S(2)}) async-start(bf16[4,12,32,2048]{3,2,1,0:T(8,128)(2,1)} %stack.2), calls=%async_computation.1 | async-start | bytes 12582912 | tf_op jit(solution)/shard_map/all_to_all | solution.py:121
  543.0 100.6 %all-gather.3.cloned.1.call-start = ((), (), s32[]{:S(2)}) async-start(), calls=%async_computation.9 | async-start | bytes 3932160 | tf_op jit(solution)/shard_map/all_gather | solution.py:131
Sparse Core Ops, SparseCore 0:
  13.3 26.0 all-reduce.3
  61.5 222.8 all-reduce.5
  288.3 84.7 all-reduce.7
  376.1 19.5 reduce-scatter.9
  397.8 83.4 reduce-scatter.5
  488.3 62.4 reduce-scatter.7
  552.3 45.7 all-gather.2
